TPU v7x, 512 devices: a whole 4x8x8 slice. The times are simulated.
512 devices in a mesh: src: 4 (over z_lo), shard: 16 (over y, core), slab: 8 (over z_hi, x).
Axes of the slice: x: 4, y: 8, z: 8 (z_hi: 2, z_lo: 4; z = z_hi * 4 + z_lo), core: 2. Of those that a mesh axis runs over, the one named last changes fastest.
Arguments:
- src_feat: bfloat16 [4, 256, 256, 256], P('src', 'slab', 'shard'), may hold values from -6 to 6
- coords: int32 [4, 2], P('src'), may hold values from 0 to 6
- offsets: int32 [8], P('slab'), may hold values from 0 to 2128
- weights: bfloat16 [4, 2, 9, 512, 128], P('src'), may hold values from -0.09375 to 0.09375
Outputs:
- target_feat: bfloat16 [4, 256, 256, 256], P('src', 'slab', 'shard')
All inputs are finite; a program needn't handle non-finite values.
Results may differ from a plain program's by a relative error of at most 0.0047.
Values may be sent and summed in bfloat16 or wider, within the bound.
A program may use at most 64 MiB of HBM per device.

v0:
```python
import math
import jax
import jax.numpy as jnp
from jax import lax
from jax.sharding import PartitionSpec as P


def with_halo(shard, sides, width):
    for axis, dim in sides:
        size, length = (lax.axis_size(axis), shard.shape[dim])
        up = [(i, (i + 1) % size) for i in range(size - 1)]
        down = [(j, i) for i, j in up]
        last = lax.slice_in_dim(shard, length - width, length, axis=dim)
        leading = lax.slice_in_dim(shard, 0, width, axis=dim)
        before = lax.ppermute(last, axis, up)
        after = lax.ppermute(leading, axis, down)
        shard = jnp.concatenate([before, shard, after], axis=dim)
    return shard


def encoding(rowpos, chan_count):
    channel_idx = jnp.arange(chan_count, dtype=jnp.int32)
    halves = (channel_idx // 2).astype(jnp.float32)
    frequency = jnp.exp(-math.log(1000.0) * halves / (chan_count / 2))
    phases = (channel_idx % 2).astype(jnp.float32) * (math.pi / 2)
    return jnp.sin(rowpos.astype(jnp.float32)[:, None] * frequency[None, :] + phases[None, :])


def blend_weights(coords):
    vertical = coords[:, 0].astype(jnp.float32) / 6.0
    across = coords[:, 1].astype(jnp.float32) / 6.0
    return jnp.stack(
        [
            (1.0 - vertical) * (1.0 - across),
            (1.0 - vertical) * across,
            vertical * (1.0 - across),
            vertical * across,
        ],
        axis=1,
    )


def local(src_feat, coords, offsets, weights):
    row_count = src_feat.shape[1]
    col_count = src_feat.shape[2]
    chan_count = src_feat.shape[3]
    rowpos = offsets[0] + jnp.arange(row_count, dtype=jnp.int32)
    encoded = encoding(rowpos, chan_count)
    posed = (src_feat.astype(jnp.float32) + encoded[None, :, None, :]).astype(jnp.bfloat16)
    all_views = lax.all_gather(posed, "src", axis=0, tiled=True)
    padded = with_halo(all_views, (("shard", 2), ("slab", 1)), 1)
    view_count = padded.shape[0]
    targets = weights.shape[0]
    groups = weights.shape[1]
    out_width = weights.shape[4]
    per_group = view_count // groups
    grouped = padded.reshape(groups, per_group, row_count + 2, col_count + 2, chan_count)
    grouped = grouped.transpose(0, 2, 3, 1, 4).reshape(
        groups, row_count + 2, col_count + 2, per_group * chan_count
    )
    convolved = jnp.zeros((targets, groups, row_count, col_count, out_width), jnp.float32)
    for tap_index in range(9):
        tap_row = tap_index // 3
        tap_col = tap_index % 3
        window = grouped[:, tap_row : tap_row + row_count, tap_col : tap_col + col_count, :]
        convolved = convolved + jnp.einsum(
            "grcn,tgno->tgrco", window, weights[:, :, tap_index], preferred_element_type=jnp.float32
        )
    convolved = convolved.transpose(0, 2, 3, 1, 4).reshape(
        targets, row_count, col_count, groups * out_width
    )
    mixing = blend_weights(coords)
    own_views = padded[:, 1:-1, 1:-1, :]
    blended = jnp.zeros((targets, row_count, col_count, chan_count), jnp.float32)
    for view_index in range(view_count):
        blended = (
            blended
            + mixing[:, view_index, None, None, None]
            * own_views[view_index].astype(jnp.float32)[None]
        )
    return (blended + jax.nn.silu(convolved)).astype(jnp.bfloat16)


def solution(mesh):
    in_specs = (
        P("src", "slab", "shard", None),
        P("src", None),
        P("slab"),
        P("src", None, None, None, None),
    )
    out_specs = P("src", "slab", "shard", None)
    return jax.shard_map(local, mesh=mesh, in_specs=in_specs, out_specs=out_specs, check_vma=False)
```

profile of v0, /device:TPU:31, one launch (start us, length us, event | category | flops | bytes accessed | tf_op | source)
XLA Modules:
  0.0 106.5 jit_solution(3161733872161110373)
XLA Ops:
  6.5 0.0 copy-start.2
  6.5 0.0 all-gather.2.cloned.1.call-start
  7.2 0.2 add_sine_fusion
  7.4 1.7 %add_convert_fusion.1 = bf16[1,32,16,256]{3,2,1,0:T(8,128)(2,1)} fusion(bf16[1,32,16,256]{3,2,1,0:T(8,128)(2,1)} %param.4, f32[32,256]{1,0:T(8,128)S(1)} %add_sine_fusion), kind=kLoop, calls=%fused_computation.22 | loop fusion | flops 393216 | bytes 557056 | tf_op jit(solution)/shard_map/convert_element_type | solution.py:49
  9.1 0.0 all-gather.2.cloned.1.call-update
  9.1 41.0 %all-gather.2.cloned.1.call-done = bf16[4,32,16,256]{3,2,1,0:T(8,128)(2,1)} async-done(((bf16[1,32,16,256]{3,2,1,0:T(8,128)(2,1)}), bf16[4,32,16,256]{3,2,1,0:T(8,128)(2,1)}) %all-gather.2.cloned.1.call-update) | async-done | bytes 1048592 | tf_op jit(solution)/shard_map/all_gather | solution.py:50
  50.2 0.0 copy-start
  50.2 1.5 %fusion.37 = (bf16[4,32,1,256]{3,2,1,0:T(2,128)(2,1)S(1)}, bf16[4,32,1,256]{3,2,1,0:T(2,128)(2,1)S(1)}) fusion(bf16[4,32,16,256]{3,2,1,0:T(8,128)(2,1)} %all-gather.2.cloned.1.call-done), kind=kLoop, calls=%fused_computation.59 | loop fusion | bytes 262144 | tf_op jit(solution)/shard_map/slice | solution.py:13
  51.7 5.1 %collective-permute-start = (bf16[4,32,1,256]{3,2,1,0:T(2,128)(2,1)S(1)}, bf16[4,32,1,256]{3,2,1,0:T(2,128)(2,1)S(1)}, u32[]{:S(2)}, u32[]{:S(2)}) collective-permute-start(bf16[4,32,1,256]{3,2,1,0:T(2,128)(2,1)S(1)} %get-tuple-element.16), channel_id=1, source_target_pairs={{0,8},{8,16},{16,24},{24,32},{32,40},{40,48},{48,56},{56,64},{64,7... | collective-permute-start | bytes 196616 | tf_op jit(solution)/shard_map/ppermute | solution.py:15
  56.8 1.9 %collective-permute-start.1 = (bf16[4,32,1,256]{3,2,1,0:T(2,128)(2,1)S(1)}, bf16[4,32,1,256]{3,2,1,0:T(2,128)(2,1)S(1)}, u32[]{:S(2)}, u32[]{:S(2)}) collective-permute-start(bf16[4,32,1,256]{3,2,1,0:T(2,128)(2,1)S(1)} %get-tuple-element.17), channel_id=1, source_target_pairs={{8,0},{16,8},{24,16},{32,24},{40,32},{48,40},{56,48},{64,56},{72,6... | collective-permute-start | bytes 196616 | tf_op jit(solution)/shard_map/ppermute | solution.py:16
  58.7 0.0 collective-permute-done
  58.7 5.6 %collective-permute-done.1 = bf16[4,32,1,256]{3,2,1,0:T(2,128)(2,1)S(1)} collective-permute-done((bf16[4,32,1,256]{3,2,1,0:T(2,128)(2,1)S(1)}, bf16[4,32,1,256]{3,2,1,0:T(2,128)(2,1)S(1)}, u32[]{:S(2)}, u32[]{:S(2)}) %collective-permute-start.1) | collective-permute-done | bytes 65568 | tf_op jit(solution)/shard_map/ppermute | solution.py:16
  64.3 0.8 pad_maximum_fusion.3
  65.1 5.3 %collective-permute-start.2 = (bf16[4,1,18,256]{3,2,1,0:T(8,128)(2,1)S(1)}, bf16[4,1,18,256]{3,2,1,0:T(8,128)(2,1)S(1)}, u32[]{:S(2)}, u32[]{:S(2)}) collective-permute-start(bf16[4,1,18,256]{3,2,1,0:T(8,128)(2,1)S(1)} %get-tuple-element.5), channel_id=1, source_target_pairs={{0,1},{1,2},{2,3},{3,4},{4,5},{5,6},{6,7},{8,9},{9,10},{10,11},{11... | collective-permute-start | bytes 110600 | tf_op jit(solution)/shard_map/ppermute | solution.py:15
  70.4 1.9 %collective-permute-start.3 = (bf16[4,1,18,256]{3,2,1,0:T(8,128)(2,1)S(1)}, bf16[4,1,18,256]{3,2,1,0:T(8,128)(2,1)S(1)}, u32[]{:S(2)}, u32[]{:S(2)}) collective-permute-start(bf16[4,1,18,256]{3,2,1,0:T(8,128)(2,1)S(1)} %get-tuple-element.6), channel_id=1, source_target_pairs={{1,0},{2,1},{3,2},{4,3},{5,4},{6,5},{7,6},{9,8},{10,9},{11,10},{12... | collective-permute-start | bytes 110600 | tf_op jit(solution)/shard_map/ppermute | solution.py:16
  72.3 0.0 copy-done.2
  72.3 0.6 fusion.38
  74.3 0.0 collective-permute-done.2
  74.3 7.0 %collective-permute-done.3 = bf16[4,1,18,256]{3,2,1,0:T(8,128)(2,1)S(1)} collective-permute-done((bf16[4,1,18,256]{3,2,1,0:T(8,128)(2,1)S(1)}, bf16[4,1,18,256]{3,2,1,0:T(8,128)(2,1)S(1)}, u32[]{:S(2)}, u32[]{:S(2)}) %collective-permute-start.3) | collective-permute-done | bytes 36896 | tf_op jit(solution)/shard_map/ppermute | solution.py:16
  81.2 0.0 copy-done
  81.2 1.1 %pad_maximum_fusion = bf16[4,34,18,256]{3,2,1,0:T(8,128)(2,1)S(1)} fusion(bf16[4,1,18,256]{3,2,1,0:T(8,128)(2,1)S(1)} %collective-permute-done.3, bf16[4,32,1,256]{3,2,1,0:T(2,128)(2,1)S(1)} %collective-permute-done.1, bf16[4,32,16,256]{3,2,1,0:T(8,128)(2,1)S(1)} %copy-done, bf16[4,32,1,256]{3,2,1,0:T(2,128)(2,1)S(1)} %collective-permute-done, ...), kind=kLoop, calls=%fused_computation | loop fusion | flops 6266880 | bytes 2506752 | tf_op jit(solution)/shard_map/concatenate | solution.py:17
  82.3 1.0 copy.130
  83.3 0.8 reshape.201
  84.2 0.0 copy-start.1
  84.2 10.1 %fusion.36 = (bf16[2,32,16,512]{3,0,2,1:T(2,128)(2,1)S(1)}, bf16[2,32,16,512]{3,0,2,1:T(2,128)(2,1)S(1)}, bf16[2,32,16,512]{3,0,2,1:T(2,128)(2,1)S(1)}, bf16[2,3...) fusion(bf16[2,34,18,512]{3,0,2,1:T(2,128)(2,1)S(1)} %reshape.201), kind=kLoop, calls=%fused_computation.58 | loop fusion | bytes 18874368 | tf_op jit(solution)/shard_map/slice | solution.py:65
  94.2 0.0 copy-done.1
  94.2 0.4 fusion.9
  94.7 0.4 convolution_add_fusion.7
  95.1 0.4 convolution_add_fusion.6
  95.6 0.4 convolution_add_fusion.5
  96.0 0.4 convolution_add_fusion.4
  96.5 0.4 convolution_add_fusion.3
  96.9 0.4 convolution_add_fusion.2
  97.4 0.4 convolution_add_fusion.1
  97.8 0.4 fusion
  98.3 0.4 copy.80
  98.7 1.0 add_convert_fusion
  (2 shorter events, 0.0 us)
Async XLA Ops:
  6.5 65.8 %copy-start.2 = (s32[1,2]{1,0:T(1,128)S(1)}, s32[1,2]{1,0:T(1,128)}, u32[]{:S(2)}) copy-start(s32[1,2]{1,0:T(1,128)} %param.5) | copy-start | bytes 28
  6.5 43.6 %all-gather.2.cloned.1.call-start = ((), (), s32[]{:S(2)}) async-start(), calls=%async_computation | async-start | bytes 1310720 | tf_op jit(solution)/shard_map/all_gather | solution.py:50
  50.2 31.0 %copy-start = (bf16[4,32,16,256]{3,2,1,0:T(8,128)(2,1)S(1)}, bf16[4,32,16,256]{3,2,1,0:T(8,128)(2,1)}, u32[]{:S(2)}) copy-start(bf16[4,32,16,256]{3,2,1,0:T(8,128)(2,1)} %all-gather.2.cloned.1.call-done) | copy-start | bytes 3145732
  51.7 7.0 %collective-permute-start = (bf16[4,32,1,256]{3,2,1,0:T(2,128)(2,1)S(1)}, bf16[4,32,1,256]{3,2,1,0:T(2,128)(2,1)S(1)}, u32[]{:S(2)}, u32[]{:S(2)}) collective-permute-start(bf16[4,32,1,256]{3,2,1,0:T(2,128)(2,1)S(1)} %get-tuple-element.16), channel_id=1, source_target_pairs={{0,8},{8,16},{16,24},{24,32},{32,40},{40,48},{48,56},{56,64},{64,7... | collective-permute-start | bytes 196616 | tf_op jit(solution)/shard_map/ppermute | solution.py:15
  56.8 7.5 %collective-permute-start.1 = (bf16[4,32,1,256]{3,2,1,0:T(2,128)(2,1)S(1)}, bf16[4,32,1,256]{3,2,1,0:T(2,128)(2,1)S(1)}, u32[]{:S(2)}, u32[]{:S(2)}) collective-permute-start(bf16[4,32,1,256]{3,2,1,0:T(2,128)(2,1)S(1)} %get-tuple-element.17), channel_id=1, source_target_pairs={{8,0},{16,8},{24,16},{32,24},{40,32},{48,40},{56,48},{64,56},{72,6... | collective-permute-start | bytes 196616 | tf_op jit(solution)/shard_map/ppermute | solution.py:16
  65.1 9.1 %collective-permute-start.2 = (bf16[4,1,18,256]{3,2,1,0:T(8,128)(2,1)S(1)}, bf16[4,1,18,256]{3,2,1,0:T(8,128)(2,1)S(1)}, u32[]{:S(2)}, u32[]{:S(2)}) collective-permute-start(bf16[4,1,18,256]{3,2,1,0:T(8,128)(2,1)S(1)} %get-tuple-element.5), channel_id=1, source_target_pairs={{0,1},{1,2},{2,3},{3,4},{4,5},{5,6},{6,7},{8,9},{9,10},{10,11},{11... | collective-permute-start | bytes 110600 | tf_op jit(solution)/shard_map/ppermute | solution.py:15
  70.4 10.9 %collective-permute-start.3 = (bf16[4,1,18,256]{3,2,1,0:T(8,128)(2,1)S(1)}, bf16[4,1,18,256]{3,2,1,0:T(8,128)(2,1)S(1)}, u32[]{:S(2)}, u32[]{:S(2)}) collective-permute-start(bf16[4,1,18,256]{3,2,1,0:T(8,128)(2,1)S(1)} %get-tuple-element.6), channel_id=1, source_target_pairs={{1,0},{2,1},{3,2},{4,3},{5,4},{6,5},{7,6},{9,8},{10,9},{11,10},{12... | collective-permute-start | bytes 110600 | tf_op jit(solution)/shard_map/ppermute | solution.py:16
  84.2 10.1 %copy-start.1 = (bf16[1,2,9,512,128]{4,3,2,1,0:T(8,128)(2,1)S(1)}, bf16[1,2,9,512,128]{4,3,2,1,0:T(8,128)(2,1)}, u32[]{:S(2)}) copy-start(bf16[1,2,9,512,128]{4,3,2,1,0:T(8,128)(2,1)} %param.7) | copy-start | bytes 7077892
Sparse Core Ops, SparseCore 0:
  9.5 40.6 all-gather.1
where the time goes:
time: 107 us
  waiting for transfers between devices  53.6 us (50%)
  between operations  15.6 us (15%)
  local copies, waits for them, and re-layouts  14.4 us (13%)
  starting transfers between devices  14.2 us (13%)
  other arithmetic  4.85 us (5%)
  matrix products  3.96 us (4%)
    all_gather x1, waiting for transfers between devices, local(): all_views = lax.all_gather(posed, 'src', axis=0, tiled=True)  41 us
    ppermute x2, waiting for transfers between devices, with_halo(): after = lax.ppermute(leading, axis, down)  12.5 us
    ppermute x2, starting transfers between devices, with_halo(): before = lax.ppermute(last, axis, up)  10.4 us
    slice x1, local copies, waits for them, and re-layouts, local(): grouped[:, tap_row:tap_row + row_count, tap_col:tap_col + col_count, :]  10.1 us
    dot_general x9, matrix products, local(): jnp.einsum('grcn,tgno->tgrco', window, weights[:, :, tap_index], preferre...  3.96 us
    ppermute x2, starting transfers between devices, with_halo(): after = lax.ppermute(leading, axis, down)  3.84 us
  transfers between devices with their start and end apart: 5, of which 3 were waited for; matrix products, arithmetic and copies ran while one was open for 1% of the time, Pallas kernels for 0%

commit v1 on v0

--- a/solution.py
+++ b/solution.py
@@ -47,7 +47,9 @@
     rowpos = offsets[0] + jnp.arange(row_count, dtype=jnp.int32)
     encoded = encoding(rowpos, chan_count)
     posed = (src_feat.astype(jnp.float32) + encoded[None, :, None, :]).astype(jnp.bfloat16)
-    all_views = lax.all_gather(posed, "src", axis=0, tiled=True)
+    all_views = jnp.concatenate(
+        lax.all_to_all(jnp.stack([posed] * lax.axis_size("src")), "src", 0, 0), axis=0
+    )
     padded = with_halo(all_views, (("shard", 2), ("slab", 1)), 1)
     view_count = padded.shape[0]
     targets = weights.shape[0]

time: 107 us -> 84.9 us (0.79)
  waiting for transfers between devices: 53.6 us -> 12.6 us
  blocking collectives: 0 us -> 31.7 us
  between operations: 15.6 us -> 2.15 us
  starting transfers between devices: 14.2 us -> 17.8 us
  other arithmetic: 4.85 us -> 3.37 us
  local copies, waits for them, and re-layouts: 14.4 us -> 13.1 us
    all_gather x1 -> x0, waiting for transfers between devices: 41 us -> none  [local(): all_views = lax.all_gather(posed, 'src', axis=0, tiled=True)]
    all_to_all x0 -> x1, blocking collectives: none -> 31.7 us  [local(): lax.all_to_all(jnp.stack([posed] * lax.axis_size('src')), 'src', 0, 0)]
    ppermute x2, starting transfers between devices: 10.4 us -> 14 us  [with_halo(): before = lax.ppermute(last, axis, up)]
    slice x1, local copies, waits for them, and re-layouts: 1.49 us -> 0.21 us  [with_halo(): last = lax.slice_in_dim(shard, length - width, length, axis=dim)]
  transfers between devices with their start and end apart: 5 -> 4, of which waited for: 3 -> 2; matrix products, arithmetic and copies ran while one was open for 1% -> 1% of each run, Pallas kernels for 0% -> 0%
where the time goes in v1:
time: 84.9 us; the launch traced here: 84.7 us
  blocking collectives  31.7 us (37%)
  starting transfers between devices  17.8 us (21%)
  local copies, waits for them, and re-layouts  13.1 us (15%)
  waiting for transfers between devices  12.6 us (15%)
  matrix products  3.96 us (5%)
  other arithmetic  3.37 us (4%)
  between operations  2.15 us (3%)
    all_to_all x1, blocking collectives, local(): lax.all_to_all(jnp.stack([posed] * lax.axis_size('src')), 'src', 0, 0)  31.7 us
    ppermute x2, starting transfers between devices, with_halo(): before = lax.ppermute(last, axis, up)  14 us
    ppermute x2, waiting for transfers between devices, with_halo(): after = lax.ppermute(leading, axis, down)  12.6 us
    slice x1, local copies, waits for them, and re-layouts, local(): grouped[:, tap_row:tap_row + row_count, tap_col:tap_col + col_count, :]  10.1 us
    dot_general x9, matrix products, local(): jnp.einsum('grcn,tgno->tgrco', window, weights[:, :, tap_index], preferre...  3.96 us
    ppermute x2, starting transfers between devices, with_halo(): after = lax.ppermute(leading, axis, down)  3.84 us
  transfers between devices with their start and end apart: 4, of which 2 were waited for; matrix products, arithmetic and copies ran while one was open for 1% of the time, Pallas kernels for 0%

profile of v1, /device:TPU:31, one launch (start us, length us, event | category | flops | bytes accessed | tf_op | source)
XLA Modules:
  0.0 84.7 jit_solution(16379567638602416921)
XLA Ops:
  0.7 0.2 add_sine_fusion
  0.9 1.0 %fusion.12 = bf16[32,16,256]{2,1,0:T(8,128)(2,1)S(1)} fusion(bf16[1,32,16,256]{3,2,1,0:T(8,128)(2,1)} %param.4, f32[32,256]{1,0:T(8,128)S(1)} %add_sine_fusion), kind=kLoop, calls=%fused_computation.24 | loop fusion | flops 393216 | bytes 557056 | tf_op jit(solution)/shard_map/convert_element_type | solution.py:49
  1.9 0.0 copy-start.1
  1.9 0.1 stack.2
  2.0 31.7 %all_to_all.5 = bf16[4,1,32,16,256]{4,3,2,1,0:T(8,128)(2,1)S(1)} all-to-all(bf16[4,1,32,16,256]{4,3,2,1,0:T(8,128)(2,1)S(1)} %stack.2), channel_id=1, replica_groups=mesh['src'=4,'shard'=16,'slab'=8] {'src'}, dimensions={0} | all-to-all | bytes 2097152 | tf_op jit(solution)/shard_map/all_to_all | solution.py:51
  33.6 0.2 fusion.39
  33.8 6.1 %collective-permute-start = (bf16[4,32,1,256]{3,2,1,0:T(2,128)(2,1)S(1)}, bf16[4,32,1,256]{3,2,1,0:T(2,128)(2,1)S(1)}, u32[]{:S(2)}, u32[]{:S(2)}) collective-permute-start(bf16[4,32,1,256]{3,2,1,0:T(2,128)(2,1)S(1)} %get-tuple-element.16), channel_id=1, source_target_pairs={{0,8},{8,16},{16,24},{24,32},{32,40},{40,48},{48,56},{56,64},{64,7... | collective-permute-start | bytes 196616 | tf_op jit(solution)/shard_map/ppermute | solution.py:15
  40.0 1.9 %collective-permute-start.1 = (bf16[4,32,1,256]{3,2,1,0:T(2,128)(2,1)S(1)}, bf16[4,32,1,256]{3,2,1,0:T(2,128)(2,1)S(1)}, u32[]{:S(2)}, u32[]{:S(2)}) collective-permute-start(bf16[4,32,1,256]{3,2,1,0:T(2,128)(2,1)S(1)} %get-tuple-element.17), channel_id=1, source_target_pairs={{8,0},{16,8},{24,16},{32,24},{40,32},{48,40},{56,48},{64,56},{72,6... | collective-permute-start | bytes 196616 | tf_op jit(solution)/shard_map/ppermute | solution.py:16
  41.9 0.0 collective-permute-done
  41.9 5.6 %collective-permute-done.1 = bf16[4,32,1,256]{3,2,1,0:T(2,128)(2,1)S(1)} collective-permute-done((bf16[4,32,1,256]{3,2,1,0:T(2,128)(2,1)S(1)}, bf16[4,32,1,256]{3,2,1,0:T(2,128)(2,1)S(1)}, u32[]{:S(2)}, u32[]{:S(2)}) %collective-permute-start.1) | collective-permute-done | bytes 65568 | tf_op jit(solution)/shard_map/ppermute | solution.py:16
  47.5 7.9 %collective-permute-start.2 = (bf16[4,1,18,256]{3,2,1,0:T(8,128)(2,1)S(1)}, bf16[4,1,18,256]{3,2,1,0:T(8,128)(2,1)S(1)}, u32[]{:S(2)}, u32[]{:S(2)}) collective-permute-start(bf16[4,1,18,256]{3,2,1,0:T(8,128)(2,1)S(1)} %get-tuple-element.5), channel_id=1, source_target_pairs={{0,1},{1,2},{2,3},{3,4},{4,5},{5,6},{6,7},{8,9},{9,10},{10,11},{11... | collective-permute-start | bytes 110600 | tf_op jit(solution)/shard_map/ppermute | solution.py:15
  55.4 1.9 %collective-permute-start.3 = (bf16[4,1,18,256]{3,2,1,0:T(8,128)(2,1)S(1)}, bf16[4,1,18,256]{3,2,1,0:T(8,128)(2,1)S(1)}, u32[]{:S(2)}, u32[]{:S(2)}) collective-permute-start(bf16[4,1,18,256]{3,2,1,0:T(8,128)(2,1)S(1)} %get-tuple-element.6), channel_id=1, source_target_pairs={{1,0},{2,1},{3,2},{4,3},{5,4},{6,5},{7,6},{9,8},{10,9},{11,10},{12... | collective-permute-start | bytes 110600 | tf_op jit(solution)/shard_map/ppermute | solution.py:16
  57.3 0.0 copy-done.1
  57.3 0.6 fusion.40
  59.2 0.0 collective-permute-done.2
  59.2 7.0 %collective-permute-done.3 = bf16[4,1,18,256]{3,2,1,0:T(8,128)(2,1)S(1)} collective-permute-done((bf16[4,1,18,256]{3,2,1,0:T(8,128)(2,1)S(1)}, bf16[4,1,18,256]{3,2,1,0:T(8,128)(2,1)S(1)}, u32[]{:S(2)}, u32[]{:S(2)}) %collective-permute-start.3) | collective-permute-done | bytes 36896 | tf_op jit(solution)/shard_map/ppermute | solution.py:16
  66.2 1.1 %pad_maximum_fusion = bf16[4,34,18,256]{3,2,1,0:T(8,128)(2,1)S(1)} fusion(bf16[4,1,18,256]{3,2,1,0:T(8,128)(2,1)S(1)} %collective-permute-done.3, bf16[4,32,1,256]{3,2,1,0:T(2,128)(2,1)S(1)} %collective-permute-done.1, bf16[4,32,16,256]{3,2,1,0:T(8,128)(2,1)S(1)} %bitcast.111, bf16[4,32,1,256]{3,2,1,0:T(2,128)(2,1)S(1)} %collective-permute-done, ...), kind=kLoop, calls=%fused_computation | loop fusion | flops 6266880 | bytes 2506752 | tf_op jit(solution)/shard_map/concatenate | solution.py:17
  67.3 1.0 %copy.129 = bf16[2,2,34,18,256]{4,1,0,3,2:T(2,128)(2,1)S(1)} copy(bf16[2,2,34,18,256]{4,3,2,1,0:T(8,128)(2,1)S(1)} %bitcast.112) | data formatting | bytes 2506752 | tf_op jit(solution)/shard_map/reshape | solution.py:59
  68.3 0.8 reshape.297
  69.2 0.0 copy-start
  69.2 10.1 %fusion.38 = (bf16[2,32,16,512]{3,0,2,1:T(2,128)(2,1)S(1)}, bf16[2,32,16,512]{3,0,2,1:T(2,128)(2,1)S(1)}, bf16[2,32,16,512]{3,0,2,1:T(2,128)(2,1)S(1)}, bf16[2,3...) fusion(bf16[2,34,18,512]{3,0,2,1:T(2,128)(2,1)S(1)} %reshape.297), kind=kLoop, calls=%fused_computation.60 | loop fusion | bytes 18874368 | tf_op jit(solution)/shard_map/slice | solution.py:67
  79.2 0.0 copy-done
  79.2 0.4 fusion.9
  79.7 0.4 convolution_add_fusion.7
  80.1 0.4 convolution_add_fusion.6
  80.6 0.4 convolution_add_fusion.5
  81.0 0.4 convolution_add_fusion.4
  81.5 0.4 convolution_add_fusion.3
  81.9 0.4 convolution_add_fusion.2
  82.4 0.4 convolution_add_fusion.1
  82.8 0.4 fusion
  83.2 0.4 copy.79
  83.7 1.0 %fusion.11 = bf16[1,32,16,256]{3,2,1,0:T(8,128)(2,1)} fusion(f32[1,32,16,256]{3,0,2,1:T(1,128)S(1)} %bitcast.114, bf16[4,1,32,16,256]{4,3,2,1,0:T(8,128)(2,1)S(1)} %all_to_all.5, f32[]{:T(128)} %bitcast.7, f32[]{:T(128)} %bitcast.6, f32[]{:T(128)} %bitcast.5, f32[]{:T(128)} %bitcast.2), kind=kLoop, calls=%fused_computation.22 | loop fusion | flops 2228224 | bytes 1835024 | tf_op jit(solution)/shard_map/convert_element_type | solution.py:83
  (3 shorter events, 0.1 us)
Async XLA Ops:
  1.9 55.4 %copy-start.1 = (s32[1,2]{1,0:T(1,128)S(1)}, s32[1,2]{1,0:T(1,128)}, u32[]{:S(2)}) copy-start(s32[1,2]{1,0:T(1,128)} %param.5) | copy-start | bytes 28
  33.8 8.0 %collective-permute-start = (bf16[4,32,1,256]{3,2,1,0:T(2,128)(2,1)S(1)}, bf16[4,32,1,256]{3,2,1,0:T(2,128)(2,1)S(1)}, u32[]{:S(2)}, u32[]{:S(2)}) collective-permute-start(bf16[4,32,1,256]{3,2,1,0:T(2,128)(2,1)S(1)} %get-tuple-element.16), channel_id=1, source_target_pairs={{0,8},{8,16},{16,24},{24,32},{32,40},{40,48},{48,56},{56,64},{64,7... | collective-permute-start | bytes 196616 | tf_op jit(solution)/shard_map/ppermute | solution.py:15
  40.0 7.5 %collective-permute-start.1 = (bf16[4,32,1,256]{3,2,1,0:T(2,128)(2,1)S(1)}, bf16[4,32,1,256]{3,2,1,0:T(2,128)(2,1)S(1)}, u32[]{:S(2)}, u32[]{:S(2)}) collective-permute-start(bf16[4,32,1,256]{3,2,1,0:T(2,128)(2,1)S(1)} %get-tuple-element.17), channel_id=1, source_target_pairs={{8,0},{16,8},{24,16},{32,24},{40,32},{48,40},{56,48},{64,56},{72,6... | collective-permute-start | bytes 196616 | tf_op jit(solution)/shard_map/ppermute | solution.py:16
  47.5 11.7 %collective-permute-start.2 = (bf16[4,1,18,256]{3,2,1,0:T(8,128)(2,1)S(1)}, bf16[4,1,18,256]{3,2,1,0:T(8,128)(2,1)S(1)}, u32[]{:S(2)}, u32[]{:S(2)}) collective-permute-start(bf16[4,1,18,256]{3,2,1,0:T(8,128)(2,1)S(1)} %get-tuple-element.5), channel_id=1, source_target_pairs={{0,1},{1,2},{2,3},{3,4},{4,5},{5,6},{6,7},{8,9},{9,10},{10,11},{11... | collective-permute-start | bytes 110600 | tf_op jit(solution)/shard_map/ppermute | solution.py:15
  55.4 10.9 %collective-permute-start.3 = (bf16[4,1,18,256]{3,2,1,0:T(8,128)(2,1)S(1)}, bf16[4,1,18,256]{3,2,1,0:T(8,128)(2,1)S(1)}, u32[]{:S(2)}, u32[]{:S(2)}) collective-permute-start(bf16[4,1,18,256]{3,2,1,0:T(8,128)(2,1)S(1)} %get-tuple-element.6), channel_id=1, source_target_pairs={{1,0},{2,1},{3,2},{4,3},{5,4},{6,5},{7,6},{9,8},{10,9},{11,10},{12... | collective-permute-start | bytes 110600 | tf_op jit(solution)/shard_map/ppermute | solution.py:16
  69.2 10.1 %copy-start = (bf16[1,2,9,512,128]{4,3,2,1,0:T(8,128)(2,1)S(1)}, bf16[1,2,9,512,128]{4,3,2,1,0:T(8,128)(2,1)}, u32[]{:S(2)}) copy-start(bf16[1,2,9,512,128]{4,3,2,1,0:T(8,128)(2,1)} %param.7) | copy-start | bytes 7077892
